TPU v7x, 32 devices: a whole 2x2x4 slice. The times are simulated.
32 devices in a mesh: ha: 8 (over y, x, core), col: 4 (over z).
Axes of the slice: x: 2, y: 2, z: 4, core: 2. Of those that a mesh axis runs over, the one named last changes fastest.
Arguments:
- features: bfloat16 [3, 32, 128, 512], P(None, 'ha', 'col'), may hold values from -18 to 18
Outputs:
- lag_cov: float32 [128, 16000], P('col', 'ha')
All inputs are finite; a program needn't handle non-finite values.
Results may differ from a plain program's by a relative error of at most 0.0003.
Values may be sent and summed in bfloat16 or wider, within the bound.
A program may use at most 384 MiB of HBM per device.

v0:
```python
import functools

import jax
import jax.numpy as jnp
from jax import lax
from jax.experimental import pallas as pl
from jax.experimental.pallas import tpu as pltpu
from jax.sharding import PartitionSpec as P

MESH = pl.DeviceIdType.MESH
REACH = 2
STEPS = 2 * REACH + 1


def window_plan(lag_count, channels, ha_count):
    share = lag_count * channels // ha_count
    spans = [-(-(i + 1) * share // channels) - i * share // channels for i in range(ha_count)]
    return share, max(spans)


def kernel(
    ha_count, col_count, x_ref, out_ref, base, stack, others, part, near, mixed, far,
    local_sem, halo_send, halo_recv, line_send, line_recv, near_send, near_recv, far_send, far_recv,
):
    frames, rows, block, width = x_ref.shape
    channels = block * col_count
    lag_count = STEPS**3
    share, span = window_plan(lag_count, channels, ha_count)
    i, j = lax.axis_index("ha"), lax.axis_index("col")
    half = ha_count // 2
    parity, place = lax.rem(i, 2), lax.div(i, 2)
    partner = i + 1 - 2 * parity

    def first_lag(index):
        return jnp.minimum(lax.div(index * share, channels), lag_count - span)

    barrier = pltpu.get_barrier_semaphore()
    for step in range(1, ha_count):
        pl.semaphore_signal(
            barrier, inc=1, device_id={"ha": lax.rem(i + step, ha_count)}, device_id_type=MESH
        )

    @pl.when(j > 0)
    def _():
        pl.semaphore_signal(barrier, inc=1, device_id={"col": j - 1}, device_id_type=MESH)

    @pl.when(j < col_count - 1)
    def _():
        pl.semaphore_signal(barrier, inc=1, device_id={"col": j + 1}, device_id_type=MESH)

    own_copies = []
    for h in range(rows):
        own_copies.append(
            pltpu.make_async_copy(
                x_ref.at[:, h], others.at[:, j, :, pl.ds(h * width, width)], local_sem.at[0, h]
            )
        )
        own_copies.append(
            pltpu.make_async_copy(
                x_ref.at[:, h], base.at[:, :, pl.ds((h + REACH) * width, width)], local_sem.at[1, h]
            )
        )
    for copy in own_copies:
        copy.start()

    ends = (j > 0).astype(jnp.int32) + (j < col_count - 1).astype(jnp.int32)
    pl.semaphore_wait(barrier, ha_count - 1 + ends)

    def halo(way, r):
        source = rows - REACH + r if way == 0 else r
        slot = r if way == 0 else rows + REACH + r
        return pltpu.make_async_remote_copy(
            src_ref=x_ref.at[:, source],
            dst_ref=base.at[:, :, pl.ds(slot * width, width)],
            send_sem=halo_send.at[way, r],
            recv_sem=halo_recv.at[way, r],
            device_id={"ha": (i + 1) if way == 0 else (i - 1)},
            device_id_type=MESH,
        )

    has_after, has_before = i < ha_count - 1, i > 0
    for way, has in ((0, has_after), (1, has_before)):

        @pl.when(has)
        def _():
            for r in range(REACH):
                halo(way, r).start()

    for copy in own_copies:
        copy.wait()

    def hop(way, step):
        sign = 1 if way == 0 else -1
        owner = j - sign * step
        return pltpu.make_async_remote_copy(
            src_ref=others.at[:, owner],
            dst_ref=others.at[:, owner],
            send_sem=line_send.at[way, step],
            recv_sem=line_recv.at[way, step],
            device_id={"col": j + sign},
            device_id_type=MESH,
        )

    def sends(way, step):
        if way == 0:
            return jnp.logical_and(j < col_count - 1, j - step >= 0)
        return jnp.logical_and(j > 0, j + step <= col_count - 1)

    def receives(way, step):
        return j - 1 - step >= 0 if way == 0 else j + 1 + step <= col_count - 1

    def arrival(way, step):
        sign = 1 if way == 0 else -1
        owner = j - sign * (step + 1)
        return pltpu.make_async_remote_copy(
            src_ref=others.at[:, owner],
            dst_ref=others.at[:, owner],
            send_sem=line_send.at[way, step],
            recv_sem=line_recv.at[way, step],
            device_id={"col": j - sign},
            device_id_type=MESH,
        )

    for way in range(2):

        @pl.when(sends(way, 0))
        def _():
            hop(way, 0).start()

    @pl.when(jnp.logical_not(has_before))
    def _():
        base[:, :, : REACH * width] = jnp.zeros((frames, block, REACH * width), base.dtype)

    @pl.when(jnp.logical_not(has_after))
    def _():
        base[:, :, (rows + REACH) * width :] = jnp.zeros((frames, block, REACH * width), base.dtype)

    for way, has_in in ((0, has_before), (1, has_after)):

        @pl.when(has_in)
        def _():
            for r in range(REACH):
                halo(way, r).wait_recv()

    column = lax.broadcasted_iota(jnp.int32, (block, width), 1)

    def shift_row(index, carry):
        t, h = lax.div(index, rows + 2 * REACH), lax.rem(index, rows + 2 * REACH)
        lanes = pl.ds(pl.multiple_of(h * width, width), width)
        plain = base[t, :, lanes]
        wide = plain.astype(jnp.float32)
        for step_w in range(STEPS):
            shift = step_w - REACH
            if shift == 0:
                stack[step_w, t, :, lanes] = plain
            else:
                moved = pltpu.roll(wide, shift % width, axis=1)
                keep = column >= shift if shift > 0 else column < width + shift
                stack[step_w, t, :, lanes] = jnp.where(keep, moved, 0.0).astype(plain.dtype)
        return carry

    lax.fori_loop(0, frames * (rows + 2 * REACH), shift_row, 0)

    for step in range(col_count - 1):
        for way in range(2):

            @pl.when(receives(way, step))
            def _():
                arrival(way, step).wait_recv()

            if step + 1 < col_count - 1:

                @pl.when(sends(way, step + 1))
                def _():
                    hop(way, step + 1).start()

    depth = rows * width
    scale = 1.0 / (frames * rows * ha_count * width)

    def products(step_h, carry):
        start = pl.multiple_of((STEPS - 1 - step_h) * width, width)
        own = stack[:, :, :, pl.ds(start, depth)].reshape(STEPS * frames * block, depth)
        field = others[...].reshape(frames * channels, depth)
        result = lax.dot_general(
            own, field, (((1,), (1,)), ((), ())), preferred_element_type=jnp.float32
        ).reshape(STEPS, frames, block, frames * channels)
        for step_w in range(STEPS):
            for step_t in range(STEPS):
                shift = step_t - REACH
                total = None
                for t in range(frames):
                    if 0 <= t + shift < frames:
                        term = result[step_w, t, :, (t + shift) * channels : (t + shift + 1) * channels]
                        total = term if total is None else total + term
                if total is None:
                    total = jnp.zeros((block, channels), jnp.float32)
                part[step_t * STEPS * STEPS + step_h * STEPS + step_w] = total * scale
        return carry

    lax.fori_loop(0, STEPS, products, 0)

    near_copies = []
    for m in range(half):
        near_copies.append(
            pltpu.make_async_remote_copy(
                src_ref=part.at[pl.ds(first_lag(2 * m + 1 - parity), span)],
                dst_ref=near.at[m],
                send_sem=near_send.at[m],
                recv_sem=near_recv.at[m],
                device_id={"ha": partner},
                device_id_type=MESH,
            )
        )
    for copy in near_copies:
        copy.start()
    far_copies = {}
    for m in range(half):
        near_copies[m].wait_recv()
        mixed[m] = part[pl.ds(first_lag(2 * m + parity), span)] + near[m]
    for r in range(1, half):
        target = lax.rem(place + r, half)
        far_copies[r] = pltpu.make_async_remote_copy(
            src_ref=mixed.at[target],
            dst_ref=far.at[r - 1],
            send_sem=far_send.at[r - 1],
            recv_sem=far_recv.at[r - 1],
            device_id={"ha": 2 * target + parity},
            device_id_type=MESH,
        )
        far_copies[r].start()
    for r in range(1, half):
        far_copies[r].wait_recv()
    for k in range(span):
        total = mixed[place, k]
        for r in range(1, half):
            total = total + far[r - 1, k]
        out_ref[:, k * channels : (k + 1) * channels] = total

    for r in range(1, half):
        far_copies[r].wait_send()
    for copy in near_copies:
        copy.wait_send()
    for step in range(col_count - 1):
        for way in range(2):

            @pl.when(sends(way, step))
            def _():
                hop(way, step).wait_send()

    for way, has in ((0, has_after), (1, has_before)):

        @pl.when(has)
        def _():
            for r in range(REACH):
                halo(way, r).wait_send()


def body(ha_count, col_count, features):
    frames, rows, block, width = features.shape
    channels = block * col_count
    lag_count = STEPS**3
    share, span = window_plan(lag_count, channels, ha_count)
    half = ha_count // 2
    dma = pltpu.SemaphoreType.DMA
    lines = max(col_count - 1, 1)
    window = pl.pallas_call(
        functools.partial(kernel, ha_count, col_count),
        out_shape=jax.ShapeDtypeStruct((block, span * channels), jnp.float32),
        in_specs=[pl.BlockSpec(memory_space=pl.ANY)],
        out_specs=pl.BlockSpec(memory_space=pltpu.VMEM),
        scratch_shapes=[
            pltpu.VMEM((frames, block, (rows + 2 * REACH) * width), features.dtype),
            pltpu.VMEM((STEPS, frames, block, (rows + 2 * REACH) * width), features.dtype),
            pltpu.VMEM((frames, col_count, block, rows * width), features.dtype),
            pltpu.VMEM((lag_count, block, channels), jnp.float32),
            pltpu.VMEM((half, span, block, channels), jnp.float32),
            pltpu.VMEM((half, span, block, channels), jnp.float32),
            pltpu.VMEM((half, span, block, channels), jnp.float32),
            dma((2, rows)),
            dma((2, REACH)),
            dma((2, REACH)),
            dma((2, lines)),
            dma((2, lines)),
            dma((half,)),
            dma((half,)),
            dma((half,)),
            dma((half,)),
        ],
        compiler_params=pltpu.CompilerParams(collective_id=0, has_side_effects=True),
        name="lag_cov",
    )(features)
    i = lax.axis_index("ha")
    first = jnp.minimum(i * share // channels, lag_count - span)
    return lax.dynamic_slice_in_dim(window, i * share - first * channels, share, 1)


def solution(mesh):
    in_specs = (P(None, "ha", "col", None),)
    out_specs = P("col", "ha")
    counts = (mesh.shape["ha"], mesh.shape["col"])
    return jax.shard_map(
        functools.partial(body, *counts), mesh=mesh, in_specs=in_specs, out_specs=out_specs, check_vma=False
    )
```

profile of v0, /device:TPU:0, one launch (start us, length us, event | category | flops | bytes accessed | tf_op | source)
XLA Modules:
  0.0 58.3 jit_solution(8863715025160107186)
XLA Ops:
  0.0 56.5 %lag_cov.1 = f32[32,2176]{1,0:T(8,128)} custom-call(bf16[3,4,32,512]{3,2,1,0:T(8,128)(2,1)} %x_ref.1), custom_call_target="tpu_custom_call" | custom-call | tf_op jit(solution)/shard_map/lag_cov/pallas_call | solution.py:266
  56.5 1.8 %constant_dynamic-slice_fusion = f32[32,2000]{1,0:T(8,128)} fusion(f32[32,2176]{1,0:T(8,128)} %lag_cov.1, s32[]{:T(128)S(6)} %select_n.9), kind=kLoop, calls=%fused_computation | loop fusion | bytes 512004 | tf_op jit(solution)/shard_map/dynamic_slice | solution.py:294
where the time goes:
time: 58.4 us; the launch traced here: 58.3 us
  Pallas kernels  56.5 us (97%)
  local copies, waits for them, and re-layouts  1.8 us (3%)
    pallas_call x1, Pallas kernels, body(): pl.pallas_call(functools.partial(kernel, ha_count, col_count), out_shape=...  56.5 us
    dynamic_slice x1, local copies, waits for them, and re-layouts, body(): lax.dynamic_slice_in_dim(window, i * share - first * channels, share, 1)  1.8 us

commit v1 on v0

--- a/solution.py
+++ b/solution.py
@@ -19,7 +19,7 @@
 
 
 def kernel(
-    ha_count, col_count, x_ref, out_ref, base, stack, others, part, near, mixed, far,
+    ha_count, col_count, x_ref, out_ref, base, stack, others, part, near, mixed, far, summed,
     local_sem, halo_send, halo_recv, line_send, line_recv, near_send, near_recv, far_send, far_recv,
 ):
     frames, rows, block, width = x_ref.shape
@@ -89,14 +89,14 @@
     for copy in own_copies:
         copy.wait()
 
-    def hop(way, step):
+    def hop(way, step, t):
         sign = 1 if way == 0 else -1
         owner = j - sign * step
         return pltpu.make_async_remote_copy(
-            src_ref=others.at[:, owner],
-            dst_ref=others.at[:, owner],
-            send_sem=line_send.at[way, step],
-            recv_sem=line_recv.at[way, step],
+            src_ref=others.at[t, owner],
+            dst_ref=others.at[t, owner],
+            send_sem=line_send.at[way, step, t],
+            recv_sem=line_recv.at[way, step, t],
             device_id={"col": j + sign},
             device_id_type=MESH,
         )
@@ -109,14 +109,14 @@
     def receives(way, step):
         return j - 1 - step >= 0 if way == 0 else j + 1 + step <= col_count - 1
 
-    def arrival(way, step):
+    def arrival(way, step, t):
         sign = 1 if way == 0 else -1
         owner = j - sign * (step + 1)
         return pltpu.make_async_remote_copy(
-            src_ref=others.at[:, owner],
-            dst_ref=others.at[:, owner],
-            send_sem=line_send.at[way, step],
-            recv_sem=line_recv.at[way, step],
+            src_ref=others.at[t, owner],
+            dst_ref=others.at[t, owner],
+            send_sem=line_send.at[way, step, t],
+            recv_sem=line_recv.at[way, step, t],
             device_id={"col": j - sign},
             device_id_type=MESH,
         )
@@ -125,7 +125,8 @@
 
         @pl.when(sends(way, 0))
         def _():
-            hop(way, 0).start()
+            for t in range(frames):
+                hop(way, 0, t).start()
 
     @pl.when(jnp.logical_not(has_before))
     def _():
@@ -161,91 +162,129 @@
 
     lax.fori_loop(0, frames * (rows + 2 * REACH), shift_row, 0)
 
-    for step in range(col_count - 1):
-        for way in range(2):
-
-            @pl.when(receives(way, step))
-            def _():
-                arrival(way, step).wait_recv()
-
-            if step + 1 < col_count - 1:
-
-                @pl.when(sends(way, step + 1))
+    def advance(step):
+        for t in range(frames):
+            for way in range(2):
+
+                @pl.when(receives(way, step))
                 def _():
-                    hop(way, step + 1).start()
+                    arrival(way, step, t).wait_recv()
+
+                if step + 1 < col_count - 1:
+
+                    @pl.when(sends(way, step + 1))
+                    def _():
+                        hop(way, step + 1, t).start()
+
+    both = jnp.minimum(j, col_count - 1 - j)
+    more_after = j < col_count - 1 - j
+
+    def owner_of(slot):
+        paired = j + ((slot + 1) // 2) * (1 if slot % 2 == 0 else -1)
+        single = jnp.where(more_after, j + (slot - both), j - (slot - both))
+        return jnp.where(slot <= 2 * both, paired, single)
 
     depth = rows * width
+    group = block // col_count
     scale = 1.0 / (frames * rows * ha_count * width)
-
-    def products(step_h, carry):
-        start = pl.multiple_of((STEPS - 1 - step_h) * width, width)
-        own = stack[:, :, :, pl.ds(start, depth)].reshape(STEPS * frames * block, depth)
-        field = others[...].reshape(frames * channels, depth)
-        result = lax.dot_general(
-            own, field, (((1,), (1,)), ((), ())), preferred_element_type=jnp.float32
-        ).reshape(STEPS, frames, block, frames * channels)
-        for step_w in range(STEPS):
-            for step_t in range(STEPS):
-                shift = step_t - REACH
-                total = None
-                for t in range(frames):
-                    if 0 <= t + shift < frames:
-                        term = result[step_w, t, :, (t + shift) * channels : (t + shift + 1) * channels]
-                        total = term if total is None else total + term
-                if total is None:
-                    total = jnp.zeros((block, channels), jnp.float32)
-                part[step_t * STEPS * STEPS + step_h * STEPS + step_w] = total * scale
-        return carry
-
-    lax.fori_loop(0, STEPS, products, 0)
-
-    near_copies = []
-    for m in range(half):
-        near_copies.append(
-            pltpu.make_async_remote_copy(
-                src_ref=part.at[pl.ds(first_lag(2 * m + 1 - parity), span)],
-                dst_ref=near.at[m],
-                send_sem=near_send.at[m],
-                recv_sem=near_recv.at[m],
+    lane_block = lax.broadcasted_iota(jnp.int32, (group, channels), 1) // block
+
+    def compute(slot):
+        owner = owner_of(slot)
+
+        def products(step_h, carry):
+            start = pl.multiple_of((STEPS - 1 - step_h) * width, width)
+            own = stack[:, :, :, pl.ds(start, depth)].reshape(STEPS * frames * block, depth)
+            field = others[:, owner].reshape(frames * block, depth)
+            result = lax.dot_general(
+                own, field, (((1,), (1,)), ((), ())), preferred_element_type=jnp.float32
+            )
+            spare = jnp.zeros((result.shape[0], channels - result.shape[1]), jnp.float32)
+            result = jnp.concatenate([result * scale, spare], axis=1)
+            moved = [result] + [pltpu.roll(result, k * block, axis=1) for k in range(1, col_count)]
+            for step_w in range(STEPS):
+                for step_t in range(STEPS):
+                    shift = step_t - REACH
+                    packed = jnp.zeros((group, channels), jnp.float32)
+                    for g in range(col_count):
+                        total = None
+                        for t in range(frames):
+                            if 0 <= t + shift < frames:
+                                row = (step_w * frames + t) * block + g * group
+                                term = moved[(g - t - shift) % col_count][row : row + group]
+                                total = term if total is None else total + term
+                        if total is not None:
+                            packed = jnp.where(lane_block == g, total, packed)
+                    part[slot, step_t * STEPS * STEPS + step_h * STEPS + step_w] = packed
+            return carry
+
+        lax.fori_loop(0, STEPS, products, 0)
+
+    near_copies, far_copies = {}, {}
+
+    def pass_near(slot):
+        for m in range(half):
+            near_copies[slot, m] = pltpu.make_async_remote_copy(
+                src_ref=part.at[slot, pl.ds(first_lag(2 * m + 1 - parity), span)],
+                dst_ref=near.at[slot, m],
+                send_sem=near_send.at[slot, m],
+                recv_sem=near_recv.at[slot, m],
                 device_id={"ha": partner},
                 device_id_type=MESH,
             )
-        )
-    for copy in near_copies:
-        copy.start()
-    far_copies = {}
-    for m in range(half):
-        near_copies[m].wait_recv()
-        mixed[m] = part[pl.ds(first_lag(2 * m + parity), span)] + near[m]
-    for r in range(1, half):
-        target = lax.rem(place + r, half)
-        far_copies[r] = pltpu.make_async_remote_copy(
-            src_ref=mixed.at[target],
-            dst_ref=far.at[r - 1],
-            send_sem=far_send.at[r - 1],
-            recv_sem=far_recv.at[r - 1],
-            device_id={"ha": 2 * target + parity},
-            device_id_type=MESH,
-        )
-        far_copies[r].start()
-    for r in range(1, half):
-        far_copies[r].wait_recv()
+            near_copies[slot, m].start()
+
+    def pass_far(slot):
+        for m in range(half):
+            near_copies[slot, m].wait_recv()
+            mixed[slot, m] = part[slot, pl.ds(first_lag(2 * m + parity), span)] + near[slot, m]
+        for r in range(1, half):
+            target = lax.rem(place + r, half)
+            far_copies[slot, r] = pltpu.make_async_remote_copy(
+                src_ref=mixed.at[slot, target],
+                dst_ref=far.at[slot, r - 1],
+                send_sem=far_send.at[slot, r - 1],
+                recv_sem=far_recv.at[slot, r - 1],
+                device_id={"ha": 2 * target + parity},
+                device_id_type=MESH,
+            )
+            far_copies[slot, r].start()
+
+    for slot in range(col_count):
+        if slot > 0:
+            advance(slot - 1)
+            pass_far(slot - 1)
+        compute(slot)
+        pass_near(slot)
+    pass_far(col_count - 1)
+
+    for slot in range(col_count):
+        for r in range(1, half):
+            far_copies[slot, r].wait_recv()
+        total = mixed[slot, place]
+        for r in range(1, half):
+            total = total + far[slot, r - 1]
+        summed[owner_of(slot)] = total
+
     for k in range(span):
-        total = mixed[place, k]
-        for r in range(1, half):
-            total = total + far[r - 1, k]
-        out_ref[:, k * channels : (k + 1) * channels] = total
-
-    for r in range(1, half):
-        far_copies[r].wait_send()
-    for copy in near_copies:
+        tiles = [summed[q, k] for q in range(col_count)]
+        for g in range(col_count):
+            rows_out = jnp.zeros((group, channels), jnp.float32)
+            for q in range(col_count):
+                turn = (q - g) * block % channels
+                tile = pltpu.roll(tiles[q], turn, axis=1) if turn else tiles[q]
+                rows_out = jnp.where(lane_block == q, tile, rows_out)
+            out_ref[g * group : (g + 1) * group, k * channels : (k + 1) * channels] = rows_out
+
+    for copy in list(far_copies.values()) + list(near_copies.values()):
         copy.wait_send()
     for step in range(col_count - 1):
         for way in range(2):
 
             @pl.when(sends(way, step))
             def _():
-                hop(way, step).wait_send()
+                for t in range(frames):
+                    hop(way, step, t).wait_send()
 
     for way, has in ((0, has_after), (1, has_before)):
 
@@ -261,6 +300,7 @@
     lag_count = STEPS**3
     share, span = window_plan(lag_count, channels, ha_count)
     half = ha_count // 2
+    group = block // col_count
     dma = pltpu.SemaphoreType.DMA
     lines = max(col_count - 1, 1)
     window = pl.pallas_call(
@@ -272,19 +312,20 @@
             pltpu.VMEM((frames, block, (rows + 2 * REACH) * width), features.dtype),
             pltpu.VMEM((STEPS, frames, block, (rows + 2 * REACH) * width), features.dtype),
             pltpu.VMEM((frames, col_count, block, rows * width), features.dtype),
-            pltpu.VMEM((lag_count, block, channels), jnp.float32),
-            pltpu.VMEM((half, span, block, channels), jnp.float32),
-            pltpu.VMEM((half, span, block, channels), jnp.float32),
-            pltpu.VMEM((half, span, block, channels), jnp.float32),
+            pltpu.VMEM((col_count, lag_count, group, channels), jnp.float32),
+            pltpu.VMEM((col_count, half, span, group, channels), jnp.float32),
+            pltpu.VMEM((col_count, half, span, group, channels), jnp.float32),
+            pltpu.VMEM((col_count, half, span, group, channels), jnp.float32),
+            pltpu.VMEM((col_count, span, group, channels), jnp.float32),
             dma((2, rows)),
             dma((2, REACH)),
             dma((2, REACH)),
-            dma((2, lines)),
-            dma((2, lines)),
-            dma((half,)),
-            dma((half,)),
-            dma((half,)),
-            dma((half,)),
+            dma((2, lines, frames)),
+            dma((2, lines, frames)),
+            dma((col_count, half)),
+            dma((col_count, half)),
+            dma((col_count, half)),
+            dma((col_count, half)),
         ],
         compiler_params=pltpu.CompilerParams(collective_id=0, has_side_effects=True),
         name="lag_cov",

time: 58.4 us -> 47.7 us (0.82)
  Pallas kernels: 56.5 us -> 45.7 us
    pallas_call x1, Pallas kernels: 56.5 us -> 45.7 us  [body(): pl.pallas_call(functools.partial(kernel, ha_count, col_count), out_shape=...]
where the time goes in v1:
time: 47.7 us; the launch traced here: 47.6 us
  Pallas kernels  45.7 us (96%)
  local copies, waits for them, and re-layouts  1.8 us (4%)
    pallas_call x1, Pallas kernels, body(): pl.pallas_call(functools.partial(kernel, ha_count, col_count), out_shape=...  45.7 us
    dynamic_slice x1, local copies, waits for them, and re-layouts, body(): lax.dynamic_slice_in_dim(window, i * share - first * channels, share, 1)  1.8 us

profile of v1, /device:TPU:0, one launch (start us, length us, event | category | flops | bytes accessed | tf_op | source)
XLA Modules:
  0.0 47.6 jit_solution(14804993973052944181)
XLA Ops:
  0.0 45.7 %lag_cov.1 = f32[32,2176]{1,0:T(8,128)} custom-call(bf16[3,4,32,512]{3,2,1,0:T(8,128)(2,1)} %x_ref.1), custom_call_target="tpu_custom_call" | custom-call | tf_op jit(solution)/shard_map/lag_cov/pallas_call | solution.py:306
  45.8 1.8 %constant_dynamic-slice_fusion = f32[32,2000]{1,0:T(8,128)} fusion(f32[32,2176]{1,0:T(8,128)} %lag_cov.1, s32[]{:T(128)S(6)} %select_n.9), kind=kLoop, calls=%fused_computation | loop fusion | bytes 512004 | tf_op jit(solution)/shard_map/dynamic_slice | solution.py:335

commit v2 on v1

--- a/solution.py
+++ b/solution.py
@@ -19,7 +19,7 @@
 
 
 def kernel(
-    ha_count, col_count, x_ref, out_ref, base, stack, others, part, near, mixed, far, summed,
+    ha_count, col_count, x_ref, out_ref, base, stack, others, part, near, mixed, far, summed, early,
     local_sem, halo_send, halo_recv, line_send, line_recv, near_send, near_recv, far_send, far_recv,
 ):
     frames, rows, block, width = x_ref.shape
@@ -52,7 +52,7 @@
     for h in range(rows):
         own_copies.append(
             pltpu.make_async_copy(
-                x_ref.at[:, h], others.at[:, j, :, pl.ds(h * width, width)], local_sem.at[0, h]
+                x_ref.at[:, h], others.at[h, j], local_sem.at[0, h]
             )
         )
         own_copies.append(
@@ -78,6 +78,45 @@
             device_id_type=MESH,
         )
 
+    def hop(way, step, h):
+        sign = 1 if way == 0 else -1
+        owner = j - sign * step
+        return pltpu.make_async_remote_copy(
+            src_ref=x_ref.at[:, h] if step == 0 else others.at[h, owner],
+            dst_ref=others.at[h, owner],
+            send_sem=line_send.at[way, step, h],
+            recv_sem=line_recv.at[way, step, h],
+            device_id={"col": j + sign},
+            device_id_type=MESH,
+        )
+
+    def sends(way, step):
+        if way == 0:
+            return jnp.logical_and(j < col_count - 1, j - step >= 0)
+        return jnp.logical_and(j > 0, j + step <= col_count - 1)
+
+    def receives(way, step):
+        return j - 1 - step >= 0 if way == 0 else j + 1 + step <= col_count - 1
+
+    def arrival(way, step, h):
+        sign = 1 if way == 0 else -1
+        owner = j - sign * (step + 1)
+        return pltpu.make_async_remote_copy(
+            src_ref=others.at[h, owner],
+            dst_ref=others.at[h, owner],
+            send_sem=line_send.at[way, step, h],
+            recv_sem=line_recv.at[way, step, h],
+            device_id={"col": j - sign},
+            device_id_type=MESH,
+        )
+
+    for way in range(2):
+
+        @pl.when(sends(way, 0))
+        def _():
+            for h in range(rows):
+                hop(way, 0, h).start()
+
     has_after, has_before = i < ha_count - 1, i > 0
     for way, has in ((0, has_after), (1, has_before)):
 
@@ -88,45 +127,6 @@
 
     for copy in own_copies:
         copy.wait()
-
-    def hop(way, step, t):
-        sign = 1 if way == 0 else -1
-        owner = j - sign * step
-        return pltpu.make_async_remote_copy(
-            src_ref=others.at[t, owner],
-            dst_ref=others.at[t, owner],
-            send_sem=line_send.at[way, step, t],
-            recv_sem=line_recv.at[way, step, t],
-            device_id={"col": j + sign},
-            device_id_type=MESH,
-        )
-
-    def sends(way, step):
-        if way == 0:
-            return jnp.logical_and(j < col_count - 1, j - step >= 0)
-        return jnp.logical_and(j > 0, j + step <= col_count - 1)
-
-    def receives(way, step):
-        return j - 1 - step >= 0 if way == 0 else j + 1 + step <= col_count - 1
-
-    def arrival(way, step, t):
-        sign = 1 if way == 0 else -1
-        owner = j - sign * (step + 1)
-        return pltpu.make_async_remote_copy(
-            src_ref=others.at[t, owner],
-            dst_ref=others.at[t, owner],
-            send_sem=line_send.at[way, step, t],
-            recv_sem=line_recv.at[way, step, t],
-            device_id={"col": j - sign},
-            device_id_type=MESH,
-        )
-
-    for way in range(2):
-
-        @pl.when(sends(way, 0))
-        def _():
-            for t in range(frames):
-                hop(way, 0, t).start()
 
     @pl.when(jnp.logical_not(has_before))
     def _():
@@ -162,19 +162,19 @@
 
     lax.fori_loop(0, frames * (rows + 2 * REACH), shift_row, 0)
 
-    def advance(step):
-        for t in range(frames):
+    def advance(step, first, last):
+        for h in range(first, last):
             for way in range(2):
 
                 @pl.when(receives(way, step))
                 def _():
-                    arrival(way, step, t).wait_recv()
+                    arrival(way, step, h).wait_recv()
 
                 if step + 1 < col_count - 1:
 
                     @pl.when(sends(way, step + 1))
                     def _():
-                        hop(way, step + 1, t).start()
+                        hop(way, step + 1, h).start()
 
     both = jnp.minimum(j, col_count - 1 - j)
     more_after = j < col_count - 1 - j
@@ -184,21 +184,28 @@
         single = jnp.where(more_after, j + (slot - both), j - (slot - both))
         return jnp.where(slot <= 2 * both, paired, single)
 
-    depth = rows * width
     group = block // col_count
     scale = 1.0 / (frames * rows * ha_count * width)
     lane_block = lax.broadcasted_iota(jnp.int32, (group, channels), 1) // block
 
-    def compute(slot):
+    def compute(slot, first, last):
+        depth = (last - first) * width
         owner = owner_of(slot)
 
         def products(step_h, carry):
-            start = pl.multiple_of((STEPS - 1 - step_h) * width, width)
+            start = pl.multiple_of((STEPS - 1 - step_h + first) * width, width)
             own = stack[:, :, :, pl.ds(start, depth)].reshape(STEPS * frames * block, depth)
-            field = others[:, owner].reshape(frames * block, depth)
+            field = jnp.concatenate(
+                [others[h, owner].reshape(frames * block, width) for h in range(first, last)], axis=1
+            )
             result = lax.dot_general(
                 own, field, (((1,), (1,)), ((), ())), preferred_element_type=jnp.float32
             )
+            if last < rows:
+                early[step_h] = result
+                return carry
+            if first > 0:
+                result = result + early[step_h]
             spare = jnp.zeros((result.shape[0], channels - result.shape[1]), jnp.float32)
             result = jnp.concatenate([result * scale, spare], axis=1)
             moved = [result] + [pltpu.roll(result, k * block, axis=1) for k in range(1, col_count)]
@@ -222,46 +229,57 @@
 
     near_copies, far_copies = {}, {}
 
+    turns = [*range(1, half), 0]
+
     def pass_near(slot):
-        for m in range(half):
-            near_copies[slot, m] = pltpu.make_async_remote_copy(
-                src_ref=part.at[slot, pl.ds(first_lag(2 * m + 1 - parity), span)],
-                dst_ref=near.at[slot, m],
-                send_sem=near_send.at[slot, m],
-                recv_sem=near_recv.at[slot, m],
+        for r in turns:
+            target = lax.rem(place + r, half)
+            near_copies[slot, r] = pltpu.make_async_remote_copy(
+                src_ref=part.at[slot, pl.ds(first_lag(2 * target + 1 - parity), span)],
+                dst_ref=near.at[slot, r],
+                send_sem=near_send.at[slot, r],
+                recv_sem=near_recv.at[slot, r],
                 device_id={"ha": partner},
                 device_id_type=MESH,
             )
-            near_copies[slot, m].start()
+            near_copies[slot, r].start()
 
     def pass_far(slot):
-        for m in range(half):
-            near_copies[slot, m].wait_recv()
-            mixed[slot, m] = part[slot, pl.ds(first_lag(2 * m + parity), span)] + near[slot, m]
-        for r in range(1, half):
+        for r in turns:
             target = lax.rem(place + r, half)
-            far_copies[slot, r] = pltpu.make_async_remote_copy(
-                src_ref=mixed.at[slot, target],
-                dst_ref=far.at[slot, r - 1],
-                send_sem=far_send.at[slot, r - 1],
-                recv_sem=far_recv.at[slot, r - 1],
-                device_id={"ha": 2 * target + parity},
-                device_id_type=MESH,
-            )
-            far_copies[slot, r].start()
-
+            near_copies[slot, r].wait_recv()
+            mixed[slot, r] = part[slot, pl.ds(first_lag(2 * target + parity), span)] + near[slot, r]
+            if r > 0:
+                far_copies[slot, r] = pltpu.make_async_remote_copy(
+                    src_ref=mixed.at[slot, r],
+                    dst_ref=far.at[slot, r - 1],
+                    send_sem=far_send.at[slot, r - 1],
+                    recv_sem=far_recv.at[slot, r - 1],
+                    device_id={"ha": 2 * target + parity},
+                    device_id_type=MESH,
+                )
+                far_copies[slot, r].start()
+
+    middle = rows // 2
     for slot in range(col_count):
-        if slot > 0:
-            advance(slot - 1)
+        if slot == col_count - 1 and slot > 0 and middle > 0:
+            advance(slot - 1, 0, middle)
             pass_far(slot - 1)
-        compute(slot)
+            compute(slot, 0, middle)
+            advance(slot - 1, middle, rows)
+            compute(slot, middle, rows)
+        else:
+            if slot > 0:
+                advance(slot - 1, 0, rows)
+                pass_far(slot - 1)
+            compute(slot, 0, rows)
         pass_near(slot)
     pass_far(col_count - 1)
 
     for slot in range(col_count):
         for r in range(1, half):
             far_copies[slot, r].wait_recv()
-        total = mixed[slot, place]
+        total = mixed[slot, 0]
         for r in range(1, half):
             total = total + far[slot, r - 1]
         summed[owner_of(slot)] = total
@@ -283,8 +301,8 @@
 
             @pl.when(sends(way, step))
             def _():
-                for t in range(frames):
-                    hop(way, step, t).wait_send()
+                for h in range(rows):
+                    hop(way, step, h).wait_send()
 
     for way, has in ((0, has_after), (1, has_before)):
 
@@ -311,17 +329,18 @@
         scratch_shapes=[
             pltpu.VMEM((frames, block, (rows + 2 * REACH) * width), features.dtype),
             pltpu.VMEM((STEPS, frames, block, (rows + 2 * REACH) * width), features.dtype),
-            pltpu.VMEM((frames, col_count, block, rows * width), features.dtype),
+            pltpu.VMEM((rows, col_count, frames, block, width), features.dtype),
             pltpu.VMEM((col_count, lag_count, group, channels), jnp.float32),
             pltpu.VMEM((col_count, half, span, group, channels), jnp.float32),
             pltpu.VMEM((col_count, half, span, group, channels), jnp.float32),
             pltpu.VMEM((col_count, half, span, group, channels), jnp.float32),
             pltpu.VMEM((col_count, span, group, channels), jnp.float32),
+            pltpu.VMEM((STEPS, STEPS * frames * block, frames * block), jnp.float32),
             dma((2, rows)),
             dma((2, REACH)),
             dma((2, REACH)),
-            dma((2, lines, frames)),
-            dma((2, lines, frames)),
+            dma((2, lines, rows)),
+            dma((2, lines, rows)),
             dma((col_count, half)),
             dma((col_count, half)),
             dma((col_count, half)),

time: 47.7 us -> 47.2 us (0.990)
  no operation moved by 1% of the time
where the time goes in v2:
time: 47.2 us; the launch traced here: 47.1 us
  Pallas kernels  45.3 us (96%)
  local copies, waits for them, and re-layouts  1.8 us (4%)
    pallas_call x1, Pallas kernels, body(): pl.pallas_call(functools.partial(kernel, ha_count, col_count), out_shape=...  45.3 us
    dynamic_slice x1, local copies, waits for them, and re-layouts, body(): lax.dynamic_slice_in_dim(window, i * share - first * channels, share, 1)  1.8 us

profile of v2, /device:TPU:0, one launch (start us, length us, event | category | flops | bytes accessed | tf_op | source)
XLA Modules:
  0.0 47.1 jit_solution(8810493355134667770)
XLA Ops:
  0.0 45.3 %lag_cov.1 = f32[32,2176]{1,0:T(8,128)} custom-call(bf16[3,4,32,512]{3,2,1,0:T(8,128)(2,1)} %x_ref.1), custom_call_target="tpu_custom_call" | custom-call | tf_op jit(solution)/shard_map/lag_cov/pallas_call | solution.py:324
  45.3 1.8 %constant_dynamic-slice_fusion = f32[32,2000]{1,0:T(8,128)} fusion(f32[32,2176]{1,0:T(8,128)} %lag_cov.1, s32[]{:T(128)S(6)} %select_n.9), kind=kLoop, calls=%fused_computation | loop fusion | bytes 512004 | tf_op jit(solution)/shard_map/dynamic_slice | solution.py:354

commit v3 on v2

--- a/solution.py
+++ b/solution.py
@@ -201,11 +201,11 @@
             result = lax.dot_general(
                 own, field, (((1,), (1,)), ((), ())), preferred_element_type=jnp.float32
             )
+            if first > 0:
+                result = result + early[step_h]
             if last < rows:
                 early[step_h] = result
                 return carry
-            if first > 0:
-                result = result + early[step_h]
             spare = jnp.zeros((result.shape[0], channels - result.shape[1]), jnp.float32)
             result = jnp.concatenate([result * scale, spare], axis=1)
             moved = [result] + [pltpu.roll(result, k * block, axis=1) for k in range(1, col_count)]
@@ -260,19 +260,24 @@
                 )
                 far_copies[slot, r].start()
 
-    middle = rows // 2
+    cuts = sorted({0, rows // 2, rows - 1, rows})
+    if col_count > 1:
+        advance(0, 0, rows)
     for slot in range(col_count):
-        if slot == col_count - 1 and slot > 0 and middle > 0:
-            advance(slot - 1, 0, middle)
+        if slot < 2:
+            compute(slot, 0, rows)
+            if slot > 0:
+                pass_far(slot - 1)
+        elif slot < col_count - 1:
+            advance(slot - 1, 0, rows)
             pass_far(slot - 1)
-            compute(slot, 0, middle)
-            advance(slot - 1, middle, rows)
-            compute(slot, middle, rows)
+            compute(slot, 0, rows)
         else:
-            if slot > 0:
-                advance(slot - 1, 0, rows)
-                pass_far(slot - 1)
-            compute(slot, 0, rows)
+            for first, last in zip(cuts, cuts[1:]):
+                advance(slot - 1, first, last)
+                if first == 0:
+                    pass_far(slot - 1)
+                compute(slot, first, last)
         pass_near(slot)
     pass_far(col_count - 1)
 

time: 47.2 us -> 44.9 us (0.951)
  Pallas kernels: 45.3 us -> 43 us
    pallas_call x1, Pallas kernels: 45.3 us -> 43 us  [body(): pl.pallas_call(functools.partial(kernel, ha_count, col_count), out_shape=...]
where the time goes in v3:
time: 44.9 us; the launch traced here: 44.8 us
  Pallas kernels  43 us (96%)
  local copies, waits for them, and re-layouts  1.8 us (4%)
    pallas_call x1, Pallas kernels, body(): pl.pallas_call(functools.partial(kernel, ha_count, col_count), out_shape=...  43 us
    dynamic_slice x1, local copies, waits for them, and re-layouts, body(): lax.dynamic_slice_in_dim(window, i * share - first * channels, share, 1)  1.8 us

profile of v3, /device:TPU:0, one launch (start us, length us, event | category | flops | bytes accessed | tf_op | source)
XLA Modules:
  0.0 44.8 jit_solution(10189353918261410265)
XLA Ops:
  0.0 43.0 %lag_cov.1 = f32[32,2176]{1,0:T(8,128)} custom-call(bf16[3,4,32,512]{3,2,1,0:T(8,128)(2,1)} %x_ref.1), custom_call_target="tpu_custom_call" | custom-call | tf_op jit(solution)/shard_map/lag_cov/pallas_call | solution.py:329
  43.0 1.8 %constant_dynamic-slice_fusion = f32[32,2000]{1,0:T(8,128)} fusion(f32[32,2176]{1,0:T(8,128)} %lag_cov.1, s32[]{:T(128)S(6)} %select_n.9), kind=kLoop, calls=%fused_computation | loop fusion | bytes 512004 | tf_op jit(solution)/shard_map/dynamic_slice | solution.py:359

commit v4 on v3

--- a/solution.py
+++ b/solution.py
@@ -110,20 +110,20 @@
             device_id_type=MESH,
         )
 
+    has_after, has_before = i < ha_count - 1, i > 0
+    for way, has in ((0, has_after), (1, has_before)):
+
+        @pl.when(has)
+        def _():
+            for r in range(REACH):
+                halo(way, r).start()
+
     for way in range(2):
 
         @pl.when(sends(way, 0))
         def _():
             for h in range(rows):
                 hop(way, 0, h).start()
-
-    has_after, has_before = i < ha_count - 1, i > 0
-    for way, has in ((0, has_after), (1, has_before)):
-
-        @pl.when(has)
-        def _():
-            for r in range(REACH):
-                halo(way, r).start()
 
     for copy in own_copies:
         copy.wait()

time: 44.9 us -> 45.1 us (level)
  no operation moved by 1% of the time
where the time goes in v4:
time: 45.1 us; the launch traced here: 45 us
  Pallas kernels  43.2 us (96%)
  local copies, waits for them, and re-layouts  1.8 us (4%)
    pallas_call x1, Pallas kernels, body(): pl.pallas_call(functools.partial(kernel, ha_count, col_count), out_shape=...  43.2 us
    dynamic_slice x1, local copies, waits for them, and re-layouts, body(): lax.dynamic_slice_in_dim(window, i * share - first * channels, share, 1)  1.8 us

profile of v4, /device:TPU:0, one launch (start us, length us, event | category | flops | bytes accessed | tf_op | source)
XLA Modules:
  0.0 45.0 jit_solution(4197186063677001673)
XLA Ops:
  0.0 43.2 %lag_cov.1 = f32[32,2176]{1,0:T(8,128)} custom-call(bf16[3,4,32,512]{3,2,1,0:T(8,128)(2,1)} %x_ref.1), custom_call_target="tpu_custom_call" | custom-call | tf_op jit(solution)/shard_map/lag_cov/pallas_call | solution.py:329
  43.2 1.8 %constant_dynamic-slice_fusion = f32[32,2000]{1,0:T(8,128)} fusion(f32[32,2176]{1,0:T(8,128)} %lag_cov.1, s32[]{:T(128)S(6)} %select_n.9), kind=kLoop, calls=%fused_computation | loop fusion | bytes 512004 | tf_op jit(solution)/shard_map/dynamic_slice | solution.py:359
